TPU v7x, 32 devices: a whole 2x2x4 slice. The times are simulated.
32 devices in a mesh: group: 4 (over z), local: 8 (over y, x, core).
Axes of the slice: x: 2, y: 2, z: 4, core: 2. Of those that a mesh axis runs over, the one named last changes fastest.
Arguments:
- tokens: bfloat16 [4096, 4096], P(('group', 'local')), may hold values from -6 to 6
- expert_ids: int32 [4096, 8], P(('group', 'local')), may hold values from 0 to 31, all different within a row; in each aligned block of 128 rows (0 to 127, 128 to 255, ...) at most 40 rows name the same one
- combine: float32 [4096, 8], P(('group', 'local')), may hold values from 0.02 to 0.5
- gate_w: bfloat16 [32, 4096, 768], P(('group', 'local')), may hold values from -0.09375 to 0.09375
- up_w: bfloat16 [32, 4096, 768], P(('group', 'local')), may hold values from -0.09375 to 0.09375
- down_w: bfloat16 [32, 768, 4096], P(('group', 'local')), may hold values from -0.21875 to 0.21875
Outputs:
- mixed: bfloat16 [4096, 4096], P(('group', 'local'))
Inputs may be any that keep to these rules, and one draw needn't show every extreme that they name: `expert_ids`: each token names 8 different experts; among the 128 tokens of one device (aligned blocks) no expert is named more than 40 times, a bound that some block reaches.
All inputs are finite; a program needn't handle non-finite values.
Results may differ from a plain program's by a relative error of at most 0.0057.
Values may be sent and summed in bfloat16 or wider, within the bound.
A program may use at most 128 MiB of HBM per device.

v0:
```python
import jax
import jax.numpy as jnp
from jax import lax
from jax.sharding import PartitionSpec as P


def local(tokens, expert_ids, combine, gate_w, up_w, down_w):
    rows_here = tokens.shape[0]
    features = tokens.shape[1]
    picks = expert_ids.shape[1]
    groups = lax.axis_size("group")
    members = lax.axis_size("local")
    experts = groups * members
    capacity = max(2, rows_here * picks * 5 // (4 * experts))
    flat_ids = expert_ids.reshape(-1)
    one_hot = (flat_ids[:, None] == jnp.arange(experts, dtype=jnp.int32)[None, :]).astype(jnp.int32)
    slot_index = jnp.sum((jnp.cumsum(one_hot, axis=0) - one_hot) * one_hot, axis=1)
    position = flat_ids * capacity + slot_index
    token_of = jnp.arange(rows_here * picks, dtype=jnp.int32) // picks
    outgoing = (
        jnp.zeros((experts * capacity, features), jnp.bfloat16).at[position].set(tokens[token_of])
    )
    arrived = lax.all_to_all(
        outgoing.reshape(experts, capacity, features),
        ("group", "local"),
        split_axis=0,
        concat_axis=0,
        tiled=True,
    )
    expert_rows = arrived.reshape(-1, features)
    gate_part = jnp.dot(expert_rows, gate_w[0], preferred_element_type=jnp.float32)
    up_part = jnp.dot(expert_rows, up_w[0], preferred_element_type=jnp.float32)
    hidden = (jax.nn.silu(gate_part) * up_part).astype(jnp.bfloat16)
    result = jnp.dot(hidden, down_w[0], preferred_element_type=jnp.float32).astype(jnp.bfloat16)
    returned = lax.all_to_all(
        result.reshape(arrived.shape), ("group", "local"), split_axis=0, concat_axis=0, tiled=True
    )
    picked = returned.reshape(experts * capacity, features)[position].reshape(
        rows_here, picks, features
    )
    total = jnp.zeros((rows_here, features), jnp.float32)
    for which in range(picks):
        total = total + combine[:, which : which + 1] * picked[:, which, :].astype(jnp.float32)
    return total.astype(jnp.bfloat16)


def solution(mesh):
    placed = (
        P(("group", "local"), None),
        P(("group", "local"), None),
        P(("group", "local"), None),
        P(("group", "local"), None, None),
        P(("group", "local"), None, None),
        P(("group", "local"), None, None),
    )
    return jax.shard_map(
        local, mesh=mesh, in_specs=placed, out_specs=P(("group", "local"), None), check_vma=False
    )
```

profile of v0, /device:TPU:0, one launch (start us, length us, event | category | flops | bytes accessed | tf_op | source)
XLA Modules:
  0.0 624.2 jit_solution(9711309624082091242)
XLA Ops:
  0.0 0.0 copy-start
  0.0 0.9 copy.16
  0.9 0.1 eq.29
  1.0 0.1 eq.25
  1.1 0.7 broadcast_multiply_fusion
  1.8 9.0 %reduce-window.6 = s32[32,8,128]{2,1,0:T(8,128)S(1)} reduce-window(s32[32,8,128]{2,1,0:T(8,128)S(1)} %fusion.24, s32[]{:T(128)} %constant.27.clone.1), window={size=1x1x128 pad=0_0x0_0x127_0}, to_apply=%region_0.0 | reduce-window | flops 4161536 | bytes 262148 | tf_op jit(solution)/shard_map/reduce-window
  10.8 0.1 slice.76
  10.9 0.1 copy.18
  11.1 0.1 copy.19
  11.1 0.1 broadcast_add_fusion
  11.3 0.1 copy.15
  11.4 0.1 mul.110
  11.5 0.0 copy-done
  11.5 7.7 %gather_fusion = bf16[1024,4096]{1,0:T(8,128)(2,1)} fusion(bf16[128,4096]{1,0:T(8,128)(2,1)S(1)} %copy-done, s32[1024]{0:T(1024)S(1)} %broadcast_clamp_fusion.1), kind=kCustom, calls=%fused_computation | custom fusion | bytes 16781312 | tf_op jit(solution)/shard_map/gather | solution.py:21
  19.3 19.0 %scatter_custom_fusion = bf16[1280,4096]{1,0:T(8,128)(2,1)} fusion(s32[1024]{0:T(1024)S(1)} %bitcast.106, bf16[1024,4096]{1,0:T(8,128)(2,1)} %gather_fusion, bf16[]{:T(256)} %constant.25.clone.1), kind=kCustom, calls=%fused_computation.9 | custom fusion | bytes 10486272 | tf_op jit(solution)/shard_map/scatter | solution.py:21
  38.2 0.0 slice-start
  38.3 0.0 slice-start.2
  38.3 235.8 %all_to_all.10 = bf16[32,40,4096]{2,1,0:T(8,128)(2,1)S(1)} all-to-all(bf16[32,40,4096]{2,1,0:T(8,128)(2,1)} %bitcast.99), channel_id=1, replica_groups=mesh['group'=4,'local'=8] {'group','local'}, dimensions={0} | all-to-all | bytes 20971520 | tf_op jit(solution)/shard_map/all_to_all | solution.py:23
  274.1 0.0 slice-start.1
  274.1 0.0 slice-start.3
  274.1 11.9 %fusion.3 = f32[1280,768]{1,0:T(8,128)} fusion(bf16[1280,4096]{1,0:T(8,128)(2,1)S(1)} %bitcast.101, bf16[1,4096,768]{2,1,0:T(8,128)(2,1)} %param.9), kind=kOutput, calls=%fused_computation.7 | convolution fusion | flops 8053063680 | bytes 20709376 | tf_op jit(solution)/shard_map/dot_general | solution.py:31
  285.9 0.0 slice-done
  285.9 0.0 slice-done.1
  285.9 10.3 %fusion.10 = bf16[1280,768]{1,0:T(8,128)(2,1)S(1)} fusion(bf16[1280,4096]{1,0:T(8,128)(2,1)S(1)} %bitcast.102, bf16[1,4096,768]{2,1,0:T(8,128)(2,1)S(1)} %bitcast.110, f32[1280,768]{1,0:T(8,128)} %fusion.3), kind=kOutput, calls=%fused_computation.12 | convolution fusion | flops 8058961920 | bytes 22675456 | tf_op jit(solution)/shard_map/dot_general | solution.py:32
  296.2 0.0 slice-done.2
  296.2 0.0 slice-done.3
  296.2 10.6 %convolution_convert_fusion = bf16[1280,4096]{1,0:T(8,128)(2,1)} fusion(bf16[1280,768]{1,0:T(8,128)(2,1)S(1)} %fusion.10, bf16[1,768,4096]{2,1,0:T(8,128)(2,1)S(1)} %bitcast.112), kind=kOutput, calls=%fused_computation.3 | convolution fusion | flops 8058306560 | bytes 18743296 | tf_op jit(solution)/shard_map/dot_general | solution.py:34
  306.8 0.0 copy-start.2
  306.8 4.3 all-to-all-start.1
  311.1 0.0 copy-done.2
  311.1 232.2 %all-to-all-done.1 = bf16[32,40,4096]{2,1,0:T(8,128)(2,1)} async-done(((bf16[32,40,4096]{2,1,0:T(8,128)(2,1)}), bf16[32,40,4096]{2,1,0:T(8,128)(2,1)}, u32[]{:S(2)}, u32[]{:S(2)}) %all-to-all-start.1) | async-done | bytes 10485792 | tf_op jit(solution)/shard_map/all_to_all | solution.py:35
  543.3 20.4 %gather_fusion.1 = bf16[1024,4096]{1,0:T(8,128)(2,1)} fusion(bf16[1280,4096]{1,0:T(8,128)(2,1)} %bitcast.12, s32[1024]{0:T(1024)S(1)} %broadcast_clamp_fusion), kind=kCustom, calls=%fused_computation.1 | custom fusion | bytes 16781312 | tf_op jit(solution)/shard_map/gather | solution.py:38
  563.8 39.3 %fusion.25 = (bf16[128,1,4096]{2,1,0:T(2,128)(2,1)S(1)}, bf16[128,1,4096]{2,1,0:T(2,128)(2,1)S(1)}, bf16[128,1,4096]{2,1,0:T(2,128)(2,1)S(1)}, bf16[128,1,4096]{...) fusion(bf16[128,8,4096]{2,1,0:T(8,128)(2,1)} %bitcast.98), kind=kLoop, calls=%fused_computation.62 | loop fusion | bytes 16777216 | tf_op jit(solution)/shard_map/slice | solution.py:43
  603.1 0.0 copy-start.1
  603.1 20.7 %fusion.14 = bf16[128,4096]{1,0:T(8,128)(2,1)} fusion(bf16[128,1,4096]{2,1,0:T(2,128)(2,1)} %get-tuple-element.12, bf16[128,1,4096]{2,1,0:T(2,128)(2,1)S(1)} %get-tuple-element.6, bf16[128,1,4096]{2,1,0:T(2,128)(2,1)S(1)} %get-tuple-element.7, bf16[128,1,4096]{2,1,0:T(2,128)(2,1)S(1)} %get-tuple-element.8, bf16[128,1,4096]{2,1,0:T(2,128)(2,1)} %get-tuple-element.9, ...), kind=kLoop, calls=%fused_computation.15 | loop fusion | flops 12582912 | bytes 9441280 | tf_op jit(solution)/shard_map/convert_element_type | solution.py:44
  623.8 0.0 copy-done.1
  (11 shorter events, 0.1 us)
Async XLA Ops:
  0.0 11.5 %copy-start = (bf16[128,4096]{1,0:T(8,128)(2,1)S(1)}, bf16[128,4096]{1,0:T(8,128)(2,1)}, u32[]{:S(2)}) copy-start(bf16[128,4096]{1,0:T(8,128)(2,1)} %param.6) | copy-start | bytes 3145732
  38.2 247.7 %slice-start = ((s8[6291456]{0:T(1024)(128)(4,1)}), s8[4194304]{0:T(1024)(128)(4,1)S(1)}, s32[]{:S(2)}) async-start(s8[6291456]{0:T(1024)(128)(4,1)} %bitcast.109), calls=%async_computation.2 | async-start | bytes 8388608
  38.3 258.0 %slice-start.2 = ((s8[6291456]{0:T(1024)(128)(4,1)}), s8[4194304]{0:T(1024)(128)(4,1)S(1)}, s32[]{:S(2)}) async-start(s8[6291456]{0:T(1024)(128)(4,1)} %bitcast.111), calls=%async_computation.4 | async-start | bytes 8388608
  274.1 11.9 %slice-start.1 = ((s8[6291456]{0:T(1024)(128)(4,1)}), s8[2097152]{0:T(1024)(128)(4,1)S(1)}, s32[]{:S(2)}) async-start(s8[6291456]{0:T(1024)(128)(4,1)} %bitcast.109), calls=%async_computation.3 | async-start | bytes 4194304
  274.1 22.2 %slice-start.3 = ((s8[6291456]{0:T(1024)(128)(4,1)}), s8[2097152]{0:T(1024)(128)(4,1)S(1)}, s32[]{:S(2)}) async-start(s8[6291456]{0:T(1024)(128)(4,1)} %bitcast.111), calls=%async_computation.5 | async-start | bytes 4194304
  306.8 4.3 copy-start.2
  306.8 236.5 %all-to-all-start.1 = ((bf16[32,40,4096]{2,1,0:T(8,128)(2,1)}), bf16[32,40,4096]{2,1,0:T(8,128)(2,1)}, u32[]{:S(2)}, u32[]{:S(2)}) async-start(bf16[32,40,4096]{2,1,0:T(8,128)(2,1)} %bitcast.100), calls=%async_computation.1 | async-start | bytes 20971520 | tf_op jit(solution)/shard_map/all_to_all | solution.py:35
  603.1 20.7 %copy-start.1 = (bf16[128,4096]{1,0:T(8,128)(2,1)S(1)}, bf16[128,4096]{1,0:T(8,128)(2,1)}, u32[]{:S(2)}) copy-start(bf16[128,4096]{1,0:T(8,128)(2,1)} %param.6) | copy-start | bytes 3145732
where the time goes:
time: 631 us; the launch traced here: 624 us
  blocking collectives  236 us (37%)
  waiting for transfers between devices  232 us (37%)
  local copies, waits for them, and re-layouts  88 us (14%)
  matrix products  32.7 us (5%)
  other arithmetic  30.6 us (5%)
    all_to_all x1, blocking collectives, local(): lax.all_to_all(outgoing.reshape(experts, capacity, features), ('group', '...  236 us
    all_to_all x1, waiting for transfers between devices, local(): lax.all_to_all(result.reshape(arrived.shape), ('group', 'local'), split_a...  232 us
    slice x1, local copies, waits for them, and re-layouts, local(): picked[:, which, :].astype(jnp.float32)  39.3 us
    convert_element_type x1, other arithmetic, local(): return total.astype(jnp.bfloat16)  20.7 us
    gather x1, local copies, waits for them, and re-layouts, local(): returned.reshape(experts * capacity, features)[position]  20.4 us
    scatter x1, local copies, waits for them, and re-layouts, local(): jnp.zeros((experts * capacity, features), jnp.bfloat16).at[position]  19 us
  transfers between devices with their start and end apart: 1, of which 1 were waited for; matrix products, arithmetic and copies ran while one was open for 0% of the time, Pallas kernels for 0%

commit v1 on v0

v1 whole, which is shorter than its diff:
```python
import jax
import jax.numpy as jnp
from jax import lax
from jax.sharding import PartitionSpec as P


def routing(expert_ids, combine, experts):
    rows = expert_ids.shape[0]
    named = expert_ids.T[:, None, :] == jnp.arange(experts, dtype=jnp.int32)[None, :, None]
    member = jnp.sum(named.astype(jnp.float32), axis=0)
    weight = jnp.sum(jnp.where(named, combine.T[:, None, :], 0.0), axis=0)
    before = (jnp.arange(rows)[:, None] < jnp.arange(rows)[None, :]).astype(jnp.bfloat16)
    rank = jnp.dot(member.astype(jnp.bfloat16), before, preferred_element_type=jnp.float32)
    return jnp.where(member > 0, rank, -1.0), weight


def plain(tokens, expert_ids, combine, gate_w, up_w, down_w):
    rows, features = tokens.shape
    groups = lax.axis_size("group")
    members = lax.axis_size("local")
    experts = groups * members
    capacity = max(2, rows * expert_ids.shape[1] * 5 // (4 * experts))
    slot, weight = routing(expert_ids, combine, experts)
    table = jnp.stack([slot, weight]).reshape(2, groups, members, rows)
    table = lax.all_to_all(table, "group", split_axis=1, concat_axis=1, tiled=True)
    slot, weight = table[0], table[1]
    blocks = lax.all_gather(tokens, "group")
    picks = slot[:, :, None, :] == jnp.arange(capacity, dtype=jnp.float32)[None, None, :, None]
    chosen = jnp.einsum(
        "blct,btd->blcd", picks.astype(jnp.bfloat16), blocks, preferred_element_type=jnp.float32
    ).astype(jnp.bfloat16)
    arrived = lax.all_to_all(chosen, "local", split_axis=1, concat_axis=1, tiled=True)
    x = arrived.reshape(-1, features)
    gate_part = jnp.dot(x, gate_w[0], preferred_element_type=jnp.float32)
    up_part = jnp.dot(x, up_w[0], preferred_element_type=jnp.float32)
    hidden = (jax.nn.silu(gate_part) * up_part).astype(jnp.bfloat16)
    result = jnp.dot(hidden, down_w[0], preferred_element_type=jnp.float32).astype(jnp.bfloat16)
    returned = lax.all_to_all(
        result.reshape(arrived.shape), "local", split_axis=1, concat_axis=1, tiled=True
    ).reshape(groups, members * capacity, features)
    mix = jnp.where(picks, weight[:, :, None, :], 0.0).reshape(groups, members * capacity, rows)
    high = mix.astype(jnp.bfloat16)
    low = (mix - high.astype(jnp.float32)).astype(jnp.bfloat16)
    part = jnp.einsum("bct,bcd->btd", high, returned, preferred_element_type=jnp.float32)
    part = part + jnp.einsum("bct,bcd->btd", low, returned, preferred_element_type=jnp.float32)
    return lax.psum_scatter(part.astype(jnp.bfloat16), "group", scatter_dimension=0, tiled=False)


def solution(mesh):
    rows = P(("group", "local"), None)
    banks = P(("group", "local"), None, None)
    return jax.shard_map(
        plain,
        mesh=mesh,
        in_specs=(rows, rows, rows, banks, banks, banks),
        out_specs=rows,
        check_vma=False,
    )
```

time: 631 us -> 512 us (0.81)
  blocking collectives: 236 us -> 134 us
  local copies, waits for them, and re-layouts: 88 us -> 38.4 us
  waiting for transfers between devices: 232 us -> 263 us
  other arithmetic: 30.6 us -> 1.05 us
  matrix products: 32.7 us -> 55.6 us
  between operations: 0.61 us -> 13.5 us
    all_to_all x1, waiting for transfers between devices: 232 us -> 116 us  [plain(): lax.all_to_all(result.reshape(arrived.shape), 'local', split_axis=1, conc...]
    all_to_all x1 -> x2, blocking collectives: 236 us -> 134 us  [the longest x1 123 us: plain(): lax.all_to_all(chosen, 'local', split_axis=1, concat_axis=1, tiled=True)]
    reduce_scatter x0 -> x1, waiting for transfers between devices: none -> 73.6 us  [plain(): lax.psum_scatter(part.astype(jnp.bfloat16), 'group', scatter_dimension=0,...]
    all_gather x0 -> x1, waiting for transfers between devices: none -> 72.5 us  [plain(): blocks = lax.all_gather(tokens, 'group')]
    slice x3 -> x0, local copies, waits for them, and re-layouts: 39.5 us -> none  [the longest x1 39.3 us: local(): picked[:, which, :].astype(jnp.float32)]
    gather x2 -> x0, local copies, waits for them, and re-layouts: 28.2 us -> none  [the longest x1 20.4 us: local(): returned.reshape(experts * capacity, features)[position]]
    dot_general x3 -> x7, matrix products: 32.7 us -> 55.6 us  [the longest x1 13.5 us: plain(): jnp.dot(hidden, down_w[0], preferred_element_type=jnp.float32)]
    convert_element_type x2, other arithmetic: 20.7 us -> 0.29 us  [the longest x1 0.16 us: plain(): low = (mix - high.astype(jnp.float32)).astype(jnp.bfloat16)]
  transfers between devices with their start and end apart: 1 -> 3, of which waited for: 1 -> 3; matrix products, arithmetic and copies ran while one was open for 0% -> 0% of each run, Pallas kernels for 0% -> 0%
where the time goes in v1:
time: 512 us; the launch traced here: 511 us
  waiting for transfers between devices  263 us (51%)
  blocking collectives  134 us (26%)
  matrix products  55.6 us (11%)
  local copies, waits for them, and re-layouts  38.4 us (8%)
  between operations  13.5 us (3%)
  starting transfers between devices  5.41 us (1%)
    all_to_all x1, blocking collectives, plain(): lax.all_to_all(chosen, 'local', split_axis=1, concat_axis=1, tiled=True)  123 us
    all_to_all x1, waiting for transfers between devices, plain(): lax.all_to_all(result.reshape(arrived.shape), 'local', split_axis=1, conc...  116 us
    reduce_scatter x1, waiting for transfers between devices, plain(): lax.psum_scatter(part.astype(jnp.bfloat16), 'group', scatter_dimension=0,...  73.6 us
    all_gather x1, waiting for transfers between devices, plain(): blocks = lax.all_gather(tokens, 'group')  72.5 us
    dot_general x1, matrix products, plain(): jnp.dot(hidden, down_w[0], preferred_element_type=jnp.float32)  13.5 us
    dot_general x1, matrix products, plain(): gate_part = jnp.dot(x, gate_w[0], preferred_element_type=jnp.float32)  12.3 us
    all_to_all x1, blocking collectives, plain(): lax.all_to_all(table, 'group', split_axis=1, concat_axis=1, tiled=True)  11.8 us
    dot_general x1, matrix products, plain(): up_part = jnp.dot(x, up_w[0], preferred_element_type=jnp.float32)  11.2 us
  transfers between devices with their start and end apart: 3, of which 3 were waited for; matrix products, arithmetic and copies ran while one was open for 0% of the time, Pallas kernels for 0%

profile of v1, /device:TPU:0, one launch (start us, length us, event | category | flops | bytes accessed | tf_op | source)
XLA Modules:
  0.0 511.1 jit_solution(9812607011304934180)
XLA Ops:
  6.5 0.0 all-gather.3.cloned.1.call-start
  6.5 0.7 all-gather.3.cloned.1.call-update
  7.3 0.8 convert_reduce_fusion
  8.0 0.1 fusion.11
  8.2 11.8 %all_to_all.15 = f32[2,4,8,128]{3,2,0,1:T(8,128)S(1)} all-to-all(f32[2,4,8,128]{3,2,0,1:T(8,128)S(1)} %pad_maximum_fusion), channel_id=1, replica_groups=mesh['group'=4,'local'=8] {'group'}, dimensions={1} | all-to-all | bytes 65536 | tf_op jit(solution)/shard_map/all_to_all | solution.py:25
  19.9 72.5 %all-gather.3.cloned.1.call-done = bf16[512,4096]{1,0:T(8,128)(2,1)} async-done(((bf16[128,4096]{1,0:T(8,128)(2,1)}), bf16[512,4096]{1,0:T(8,128)(2,1)}) %all-gather.3.cloned.1.call-update) | async-done | bytes 4194320 | tf_op jit(solution)/shard_map/all_gather | solution.py:27
  92.4 7.7 %convolution_convert_fusion.1 = bf16[4,8,40,4096]{3,2,1,0:T(8,128)(2,1)} fusion(bf16[4,128,4096,1]{2,1,3,0:T(8,128)(2,1)} %bitcast.68, f32[4,8,128]{2,1,0:T(8,128)S(1)} %get-tuple-element.7), kind=kOutput, calls=%fused_computation.2 | convolution fusion | flops 1347584000 | bytes 14696448 | tf_op jit(solution)/shard_map/blct,btd->blcd/dot_general | solution.py:29
  100.1 9.5 %copy.18 = bf16[4,8,40,4096]{3,2,0,1:T(8,128)(2,1)} copy(bf16[4,8,40,4096]{3,2,1,0:T(8,128)(2,1)} %convolution_convert_fusion.1) | data formatting | bytes 20971520 | tf_op jit(solution)/shard_map/convert_element_type | solution.py:31
  109.5 122.6 %all_to_all.16 = bf16[4,8,40,4096]{3,2,0,1:T(8,128)(2,1)} all-to-all(bf16[4,8,40,4096]{3,2,0,1:T(8,128)(2,1)} %copy.18), channel_id=1, replica_groups=mesh['group'=4,'local'=8] {'local'}, dimensions={1} | all-to-all | bytes 20971520 | tf_op jit(solution)/shard_map/all_to_all | solution.py:32
  232.1 9.5 %copy.19 = bf16[4,8,40,4096]{3,2,1,0:T(8,128)(2,1)} copy(bf16[4,8,40,4096]{3,2,0,1:T(8,128)(2,1)} %all_to_all.16) | data formatting | bytes 20971520 | tf_op jit(solution)/shard_map/all_to_all | solution.py:32
  241.6 0.0 copy-start
  241.6 12.3 %fusion.3 = f32[1280,768]{1,0:T(8,128)S(1)} fusion(bf16[1280,4096]{1,0:T(8,128)(2,1)} %bitcast.65, bf16[1,4096,768]{2,1,0:T(8,128)(2,1)} %param.9), kind=kOutput, calls=%fused_computation.6 | convolution fusion | flops 8053063680 | bytes 20709376 | tf_op jit(solution)/shard_map/dot_general | solution.py:34
  253.9 0.0 copy-done
  253.9 11.2 %fusion.8 = bf16[1280,768]{1,0:T(8,128)(2,1)S(1)} fusion(bf16[1280,4096]{1,0:T(8,128)(2,1)S(1)} %bitcast.66, bf16[1,4096,768]{2,1,0:T(8,128)(2,1)} %param.10, f32[1280,768]{1,0:T(8,128)S(1)} %fusion.3), kind=kOutput, calls=%fused_computation.9 | convolution fusion | flops 8058961920 | bytes 22675456 | tf_op jit(solution)/shard_map/dot_general | solution.py:35
  265.1 13.5 %convolution_convert_fusion = bf16[1280,4096]{1,0:T(8,128)(2,1)} fusion(bf16[1280,768]{1,0:T(8,128)(2,1)S(1)} %fusion.8, bf16[1,768,4096]{2,1,0:T(8,128)(2,1)} %param.11), kind=kOutput, calls=%fused_computation | convolution fusion | flops 8058306560 | bytes 18743296 | tf_op jit(solution)/shard_map/dot_general | solution.py:37
  278.6 9.5 %copy.20 = bf16[4,8,40,4096]{3,2,0,1:T(8,128)(2,1)} copy(bf16[4,8,40,4096]{3,2,1,0:T(8,128)(2,1)} %bitcast.67) | data formatting | bytes 20971520 | tf_op jit(solution)/shard_map/reshape | solution.py:39
  288.1 5.1 %all-to-all-start.2 = ((bf16[4,8,40,4096]{3,2,0,1:T(8,128)(2,1)}), bf16[4,8,40,4096]{3,2,0,1:T(8,128)(2,1)}, u32[]{:S(2)}, u32[]{:S(2)}) async-start(bf16[4,8,40,4096]{3,2,0,1:T(8,128)(2,1)} %copy.20), calls=%async_computation.2 | async-start | bytes 20971520 | tf_op jit(solution)/shard_map/all_to_all | solution.py:38
  293.2 0.3 reduce-scatter.2.cloned.1.call-start
  293.5 0.1 eq.46
  293.6 0.2 fusion.14
  293.8 0.1 fusion.13
  293.9 115.9 %all-to-all-done.2 = bf16[4,8,40,4096]{3,2,0,1:T(8,128)(2,1)} async-done(((bf16[4,8,40,4096]{3,2,0,1:T(8,128)(2,1)}), bf16[4,8,40,4096]{3,2,0,1:T(8,128)(2,1)}, u32[]{:S(2)}, u32[]{:S(2)}) %all-to-all-start.2) | async-done | bytes 10485792 | tf_op jit(solution)/shard_map/all_to_all | solution.py:38
  409.8 9.5 %copy.21 = bf16[4,8,40,4096]{3,2,1,0:T(8,128)(2,1)} copy(bf16[4,8,40,4096]{3,2,0,1:T(8,128)(2,1)} %all-to-all-done.2) | data formatting | bytes 20971520 | tf_op jit(solution)/shard_map/all_to_all | solution.py:38
  419.2 0.0 slice-start
  419.2 0.0 slice-start.1
  419.2 0.0 slice-start.2
  419.2 6.5 %fusion.17 = f32[4,128,4096]{2,1,0:T(8,128)S(1)} fusion(bf16[4,320,128]{2,1,0:T(8,128)(2,1)S(1)} %fusion.13, bf16[4,320,4096]{2,1,0:T(8,128)(2,1)} %bitcast.61), kind=kOutput, calls=%fused_computation.27 | convolution fusion | flops 1342177280 | bytes 19202048 | tf_op jit(solution)/shard_map/bct,bcd->btd/dot_general | solution.py:44
  425.7 0.0 slice-done
  425.7 0.0 slice-done.1
  425.8 0.5 slice-done.2
  426.3 4.3 add_convert_fusion
  430.6 0.0 reduce-scatter.2.cloned.1.call-update
  430.6 73.6 %reduce-scatter.2.cloned.1.call-done = bf16[1,128,4096]{2,1,0:T(8,128)(2,1)} async-done(((bf16[4,128,4096]{2,1,0:T(8,128)(2,1)}), bf16[1,128,4096]{2,1,0:T(8,128)(2,1)}) %reduce-scatter.2.cloned.1.call-update) | async-done | bytes 1048592 | tf_op jit(solution)/shard_map/reduce_scatter | solution.py:46
  (4 shorter events, 0.0 us)
Async XLA Ops:
  6.5 85.9 %all-gather.3.cloned.1.call-start = ((), (), s32[]{:S(2)}) async-start(), calls=%async_computation.5 | async-start | bytes 5242880 | tf_op jit(solution)/shard_map/all_gather | solution.py:27
  241.6 12.3 %copy-start = (bf16[4,8,40,4096]{3,2,1,0:T(8,128)(2,1)S(1)}, bf16[4,8,40,4096]{3,2,1,0:T(8,128)(2,1)}, u32[]{:S(2)}) copy-start(bf16[4,8,40,4096]{3,2,1,0:T(8,128)(2,1)} %copy.19) | copy-start | bytes 31457284
  288.1 121.7 %all-to-all-start.2 = ((bf16[4,8,40,4096]{3,2,0,1:T(8,128)(2,1)}), bf16[4,8,40,4096]{3,2,0,1:T(8,128)(2,1)}, u32[]{:S(2)}, u32[]{:S(2)}) async-start(bf16[4,8,40,4096]{3,2,0,1:T(8,128)(2,1)} %copy.20), calls=%async_computation.2 | async-start | bytes 20971520 | tf_op jit(solution)/shard_map/all_to_all | solution.py:38
  293.2 211.1 %reduce-scatter.2.cloned.1.call-start = ((), (), s32[]{:S(2)}) async-start(), calls=%async_computation.4 | async-start | bytes 5242880 | tf_op jit(solution)/shard_map/reduce_scatter | solution.py:46
  419.2 6.5 %slice-start = ((s8[10485760]{0:T(1024)(128)(4,1)}), s8[4194304]{0:T(1024)(128)(4,1)S(1)}, s32[]{:S(2)}) async-start(s8[10485760]{0:T(1024)(128)(4,1)} %bitcast.62), calls=%async_computation.6 | async-start | bytes 8388608
  419.2 6.5 %slice-start.1 = ((s8[10485760]{0:T(1024)(128)(4,1)}), s8[4194304]{0:T(1024)(128)(4,1)S(1)}, s32[]{:S(2)}) async-start(s8[10485760]{0:T(1024)(128)(4,1)} %bitcast.62), calls=%async_computation.7 | async-start | bytes 8388608
  419.2 7.0 %slice-start.2 = ((s8[10485760]{0:T(1024)(128)(4,1)}), s8[2097152]{0:T(1024)(128)(4,1)S(1)}, s32[]{:S(2)}) async-start(s8[10485760]{0:T(1024)(128)(4,1)} %bitcast.62), calls=%async_computation.8 | async-start | bytes 4194304
Sparse Core Ops, SparseCore 0:
  8.9 83.4 all-gather.2
  430.7 73.4 reduce-scatter.1
